TPU v7x, 512 devices: a whole 4x8x8 slice. The times are simulated.
512 devices in a mesh: vocab: 64 (over x, y, core), tok: 8 (over z).
Axes of the slice: x: 4, y: 8, z: 8, core: 2. Of those that a mesh axis runs over, the one named last changes fastest.
Arguments:
- hidden: bfloat16 [1024, 3584], P('tok'), may hold values from -320 to 320
- head: bfloat16 [3584, 98304], P('tok', 'vocab'), may hold values from -2 to 2
- teacher: bfloat16 [1024, 98304], P('tok', 'vocab'), may hold values from 0 to 1, as said below
- block_ids: int32 [8, 16], P('tok'), may hold values from -1 to 191, as said below
- counts: int32 [8], P('tok'), may hold values from 8 to 16
Outputs:
- lse: float32 [1024], P('tok')
- kl: float32 [1024], P('tok')
- grad_hidden: float32 [1024, 3584], P('tok', 'vocab')
- grad_head: bfloat16 [3584, 98304], P('tok', 'vocab')
Inputs may be any that keep to these rules, and one draw needn't show every extreme that they name: `block_ids`: row b lists counts[b] distinct teacher blocks (block k covers columns 512 * k to 512 * k + 511) in its first counts[b] entries; the rest of the row is -1. `teacher`: every entry is positive.
All inputs are finite; a program needn't handle non-finite values.
Results may differ from a plain program's by a relative error of at most 0.0055.
Values may be sent and summed in bfloat16 or wider, within the bound.
A program may use at most 64 MiB of HBM per device.

v0:
```python
import jax
import jax.numpy as jnp
from jax import lax
from jax.sharding import PartitionSpec as P

BLK = 512
loss_scale = 1024.0


def local_stats(logits, teacher, listed):
    teacher_f = teacher.astype(jnp.float32)
    kept = jnp.where(listed, teacher_f, 0.0)
    local_top = jnp.max(logits, axis=1)
    local_sum = jnp.sum(jnp.exp(logits - local_top[:, None]), axis=1)
    local_mass = jnp.sum(kept, axis=1)
    local_part = jnp.sum(jnp.where(listed, teacher_f * (jnp.log(teacher_f) - logits), 0.0), axis=1)
    return (kept, (local_top, local_sum, local_mass, local_part))


def finish_stats(logits, kept, global_top, total_sum, total_mass, total_part):
    lse = global_top + jnp.log(total_sum)
    kl = total_part / total_mass - jnp.log(total_mass) + lse
    student = jnp.exp(logits - lse[:, None])
    delta = (loss_scale * (student - kept / total_mass[:, None])).astype(jnp.bfloat16)
    return (lse, kl, delta)


def listed_columns(block_ids, counts, column_block, token_count):
    live_slot = jnp.arange(block_ids.shape[1], dtype=jnp.int32)[None, :] < counts[:, None]
    block_hit = jnp.any(
        (block_ids[:, :, None] == column_block[None, None, :]) & live_slot[:, :, None], axis=1
    )
    token_blocks = block_hit.shape[0]
    width = column_block.shape[0]
    return jnp.broadcast_to(
        block_hit[:, None, :], (token_blocks, token_count // token_blocks, width)
    ).reshape(token_count, width)


def per_device(hidden, head, teacher, block_ids, counts):
    token_count = hidden.shape[0]
    column_count = head.shape[1]
    full_head = lax.all_gather(head, "tok", axis=0, tiled=True)
    logits = jnp.dot(hidden, full_head, preferred_element_type=jnp.float32)
    first_column = lax.axis_index("vocab") * column_count
    column_block = (first_column + jnp.arange(column_count, dtype=jnp.int32)) // BLK
    listed = listed_columns(block_ids, counts, column_block, token_count)
    kept, stats_here = local_stats(logits, teacher, listed)
    local_top, local_sum, local_mass, local_part = stats_here
    global_top = lax.pmax(local_top, "vocab")
    scaled_sum = local_sum * jnp.exp(local_top - global_top)
    total_sum, total_mass, total_part = lax.psum((scaled_sum, local_mass, local_part), "vocab")
    lse, kl, delta = finish_stats(logits, kept, global_top, total_sum, total_mass, total_part)
    grad_hidden = lax.psum_scatter(
        lax.dot_general(
            full_head, delta, (((1,), (1,)), ((), ())), preferred_element_type=jnp.float32
        ),
        "vocab",
        scatter_dimension=0,
        tiled=True,
    ).T
    slices = lax.all_to_all(hidden, "tok", split_axis=1, concat_axis=0, tiled=True)
    grad_head = lax.dot_general(
        slices,
        lax.all_gather(delta, "tok", axis=0, tiled=True),
        (((0,), (0,)), ((), ())),
        preferred_element_type=jnp.float32,
    ).astype(jnp.bfloat16)
    return (lse, kl, grad_hidden, grad_head)


def solution(mesh):
    placed = (P("tok", None), P("tok", "vocab"), P("tok", "vocab"), P("tok", None), P("tok"))
    return jax.shard_map(
        per_device,
        mesh=mesh,
        in_specs=placed,
        out_specs=(P("tok"), P("tok"), P("tok", "vocab"), P("tok", "vocab")),
        check_vma=False,
    )
```

profile of v0, /device:TPU:1, one launch (start us, length us, event | category | flops | bytes accessed | tf_op | source)
XLA Modules:
  0.0 657.2 jit_solution(4507832720757288670)
XLA Ops:
  7.2 0.0 all-gather.3.cloned.1.call-start
  7.2 0.7 all-gather.3.cloned.1.call-update
  7.9 0.0 all-reduce.4.cloned.1.call-start
  8.6 0.8 and_reduce_fusion
  9.4 0.0 copy-start.2
  9.4 128.1 %all-gather.3.cloned.1.call-done = bf16[3584,1536]{1,0:T(8,128)(2,1)} async-done(((bf16[448,1536]{1,0:T(8,128)(2,1)}), bf16[3584,1536]{1,0:T(8,128)(2,1)}) %all-gather.3.cloned.1.call-update) | async-done | bytes 11010064 | tf_op jit(solution)/shard_map/all_gather | solution.py:43
  137.5 6.1 fusion.14
  143.6 124.3 %pmax.7 = f32[128]{0:T(128)S(1)} all-reduce(f32[128]{0:T(128)S(1)} %get-tuple-element.28), channel_id=1, replica_groups=mesh['vocab'=64,'tok'=8] {'vocab'}, use_global_device_ids=true, to_apply=%region_1.2 | all-reduce | flops 128 | bytes 1024 | tf_op jit(solution)/shard_map/pmax | solution.py:50
  267.8 0.0 copy-done.2
  267.8 0.5 fusion.9
  268.3 128.3 %all-reduce.1 = (f32[128]{0:T(128)S(1)}, f32[128]{0:T(128)S(1)}, f32[128]{0:T(128)S(1)}) all-reduce(f32[128]{0:T(128)S(1)} %exponential_multiply_fusion, f32[128]{0:T(128)S(1)} %get-tuple-element.22, f32[128]{0:T(128)S(1)} %get-tuple-element.20), channel_id=1, replica_groups=mesh['vocab'=64,'tok'=8] {'vocab'}, use_global_device_ids=true, to_apply=%region_3.4 | all-reduce | flops 384 | bytes 3072 | tf_op jit(solution)/shard_map/psum | solution.py:52
  396.6 0.5 subtract_add_fusion
  397.1 0.0 copy-start.3
  397.1 0.3 fusion.10
  397.4 0.0 copy-start.1
  397.4 0.0 copy-start
  397.4 9.1 %convolution_bitcast_fusion = f32[3584,128]{0,1:T(8,128)} fusion(bf16[128,1536]{1,0:T(8,128)(2,1)S(1)} %fusion.10, bf16[3584,1536]{1,0:T(8,128)(2,1)} %all-gather.3.cloned.1.call-done), kind=kOutput, calls=%fused_computation | convolution fusion | flops 1409286144 | bytes 13238272 | tf_op jit(solution)/shard_map/dot_general | solution.py:55
  406.6 0.0 copy-done.3
  406.6 0.0 copy-done.1
  406.6 0.0 all-reduce.4.cloned.1.call-update
  406.6 0.0 all-gather.5.cloned.1.call-start
  406.6 0.7 all-gather.5.cloned.1.call-update
  407.3 0.0 copy-done
  407.3 1.3 copy.16
  408.6 3.8 all-to-all-start
  412.4 1.3 dynamic-slice
  414.3 182.0 %all-reduce.4.cloned.1.call-done = f32[3584,128]{0,1:T(8,128)} async-done(((f32[3584,128]{0,1:T(8,128)}), f32[3584,128]{0,1:T(8,128)}) %all-reduce.4.cloned.1.call-update) | async-done | bytes 1835024
  596.3 1.0 dynamic-slice_bitcast_fusion
  597.3 0.7 copy.18
  598.0 0.0 all-to-all-done
  598.0 48.1 %all-gather.5.cloned.1.call-done = bf16[1024,1536]{1,0:T(8,128)(2,1)} async-done(((bf16[128,1536]{1,0:T(8,128)(2,1)}), bf16[1024,1536]{1,0:T(8,128)(2,1)}) %all-gather.5.cloned.1.call-update) | async-done | bytes 3145744 | tf_op jit(solution)/shard_map/all_gather | solution.py:65
  646.1 4.6 fusion
  (3 shorter events, 0.0 us)
Async XLA Ops:
  7.2 130.3 %all-gather.3.cloned.1.call-start = ((), (), s32[]{:S(2)}) async-start(), calls=%async_computation.1 | async-start | bytes 12386304 | tf_op jit(solution)/shard_map/all_gather | solution.py:43
  7.9 588.4 %all-reduce.4.cloned.1.call-start = ((), (), s32[]{:S(2)}) async-start(), calls=%async_computation.3 | async-start | bytes 3670016
  9.4 258.5 %copy-start.2 = (bf16[128,1536]{1,0:T(8,128)(2,1)S(1)}, bf16[128,1536]{1,0:T(8,128)(2,1)}, u32[]{:S(2)}) copy-start(bf16[128,1536]{1,0:T(8,128)(2,1)} %param.7) | copy-start | bytes 1179652
  397.1 9.5 %copy-start.3 = (f32[128]{0:T(128)}, f32[128]{0:T(128)S(1)}, u32[]{:S(2)}) copy-start(f32[128]{0:T(128)S(1)} %get-tuple-element.27) | copy-start | bytes 1540
  397.4 9.2 %copy-start.1 = (bf16[128,1536]{1,0:T(8,128)(2,1)}, bf16[128,1536]{1,0:T(8,128)(2,1)S(1)}, u32[]{:S(2)}) copy-start(bf16[128,1536]{1,0:T(8,128)(2,1)S(1)} %fusion.10) | copy-start | bytes 1179652
  397.4 9.9 %copy-start = (bf16[128,3584]{1,0:T(8,128)(2,1)S(1)}, bf16[128,3584]{1,0:T(8,128)(2,1)}, u32[]{:S(2)}) copy-start(bf16[128,3584]{1,0:T(8,128)(2,1)} %param.5) | copy-start | bytes 2752516
  406.6 239.5 %all-gather.5.cloned.1.call-start = ((), (), s32[]{:S(2)}) async-start(), calls=%async_computation.2 | async-start | bytes 3538944 | tf_op jit(solution)/shard_map/all_gather | solution.py:65
  408.6 189.4 %all-to-all-start = ((bf16[128,8,448]{0,2,1:T(8,128)(2,1)}), bf16[128,8,448]{0,2,1:T(8,128)(2,1)S(1)}, u32[]{:S(2)}, u32[]{:S(2)}) async-start(bf16[128,8,448]{0,2,1:T(8,128)(2,1)} %bitcast.4), calls=%async_computation | async-start | bytes 1835008 | tf_op jit(solution)/shard_map/all_to_all | solution.py:62
Sparse Core Ops, SparseCore 0:
  10.1 127.3 all-gather.2
  406.7 189.5 all-reduce.3
  598.4 47.6 all-gather.4
where the time goes:
time: 658 us; the launch traced here: 657 us
  waiting for transfers between devices  360 us (55%)
  blocking collectives  253 us (38%)
  matrix products  19.8 us (3%)
  between operations  15.1 us (2%)
    unnamed x4, waiting for transfers between devices  183 us
    psum x1, blocking collectives, per_device(): lax.psum((scaled_sum, local_mass, local_part), 'vocab')  128 us
    all_gather x1, waiting for transfers between devices, per_device(): full_head = lax.all_gather(head, 'tok', axis=0, tiled=True)  128 us
    pmax x1, blocking collectives, per_device(): global_top = lax.pmax(local_top, 'vocab')  124 us
    all_gather x1, waiting for transfers between devices, per_device(): lax.all_gather(delta, 'tok', axis=0, tiled=True)  48.1 us
  transfers between devices with their start and end apart: 4, of which 3 were waited for; matrix products, arithmetic and copies ran while one was open for 1% of the time, Pallas kernels for 0%

commit v1 on v0

--- a/solution.py
+++ b/solution.py
@@ -5,6 +5,13 @@
 
 BLK = 512
 loss_scale = 1024.0
+
+
+def swapped_in(x, axis, d):
+    count = lax.axis_size(axis)
+    blocks = jnp.stack([x for _ in range(count)])
+    blocks = lax.all_to_all(blocks, axis, split_axis=0, concat_axis=0)
+    return jnp.concatenate(blocks, axis=d)
 
 
 def local_stats(logits, teacher, listed):
@@ -62,7 +69,7 @@
     slices = lax.all_to_all(hidden, "tok", split_axis=1, concat_axis=0, tiled=True)
     grad_head = lax.dot_general(
         slices,
-        lax.all_gather(delta, "tok", axis=0, tiled=True),
+        swapped_in(delta, "tok", 0),
         (((0,), (0,)), ((), ())),
         preferred_element_type=jnp.float32,
     ).astype(jnp.bfloat16)

time: 658 us -> 634 us (0.964)
  waiting for transfers between devices: 360 us -> 319 us
  starting transfers between devices: 3.94 us -> 15.4 us
    all_gather x1 -> x0, waiting for transfers between devices: 48.1 us -> none  [per_device(): lax.all_gather(delta, 'tok', axis=0, tiled=True)]
    unnamed x4 -> x3, waiting for transfers between devices: 183 us -> 193 us
    all_to_all x1, starting transfers between devices: 3.83 us -> 10.9 us  [per_device(): lax.all_to_all(hidden, 'tok', split_axis=1, concat_axis=0, tiled=True)]
  transfers between devices with their start and end apart: 4 -> 4, of which waited for: 3 -> 2; matrix products, arithmetic and copies ran while one was open for 1% -> 3% of each run, Pallas kernels for 0% -> 0%
where the time goes in v1:
time: 634 us; the launch traced here: 631 us
  waiting for transfers between devices  319 us (50%)
  blocking collectives  253 us (40%)
  matrix products  19.3 us (3%)
  starting transfers between devices  15.4 us (2%)
  between operations  15.4 us (2%)
  local copies, waits for them, and re-layouts  7.08 us (1%)
    unnamed x3, waiting for transfers between devices  193 us
    psum x1, blocking collectives, per_device(): lax.psum((scaled_sum, local_mass, local_part), 'vocab')  129 us
    all_gather x1, waiting for transfers between devices, per_device(): full_head = lax.all_gather(head, 'tok', axis=0, tiled=True)  127 us
    pmax x1, blocking collectives, per_device(): global_top = lax.pmax(local_top, 'vocab')  125 us
  transfers between devices with their start and end apart: 4, of which 2 were waited for; matrix products, arithmetic and copies ran while one was open for 3% of the time, Pallas kernels for 0%

profile of v1, /device:TPU:1, one launch (start us, length us, event | category | flops | bytes accessed | tf_op | source)
XLA Modules:
  0.0 631.2 jit_solution(16260579794564994188)
XLA Ops:
  7.2 0.0 copy-start
  7.2 0.0 copy-start.3
  7.2 0.0 all-gather.2.cloned.1.call-start
  7.2 0.7 all-gather.2.cloned.1.call-update
  7.9 2.2 copy.13
  10.1 10.9 %all-to-all-start.1 = ((bf16[128,8,448]{0,2,1:T(8,128)(2,1)}), bf16[128,8,448]{0,2,1:T(8,128)(2,1)S(1)}, u32[]{:S(2)}, u32[]{:S(2)}) async-start(bf16[128,8,448]{0,2,1:T(8,128)(2,1)} %bitcast.4), calls=%async_computation.1 | async-start | bytes 1835008 | tf_op jit(solution)/shard_map/all_to_all | solution.py:69
  21.7 0.0 copy-done.3
  21.7 0.1 and_reduce_fusion
  21.8 0.0 copy-start.1
  21.8 126.6 %all-gather.2.cloned.1.call-done = bf16[3584,1536]{1,0:T(8,128)(2,1)} async-done(((bf16[448,1536]{1,0:T(8,128)(2,1)}), bf16[3584,1536]{1,0:T(8,128)(2,1)}) %all-gather.2.cloned.1.call-update) | async-done | bytes 11010064 | tf_op jit(solution)/shard_map/all_gather | solution.py:50
  148.4 0.0 copy-done
  148.4 5.8 fusion.14
  154.2 124.7 %pmax.7 = f32[128]{0:T(128)S(1)} all-reduce(f32[128]{0:T(128)S(1)} %get-tuple-element.24), channel_id=1, replica_groups=mesh['vocab'=64,'tok'=8] {'vocab'}, use_global_device_ids=true, to_apply=%region_1.2 | all-reduce | flops 128 | bytes 1024 | tf_op jit(solution)/shard_map/pmax | solution.py:57
  278.9 0.0 copy-done.1
  278.9 0.5 fusion.9
  279.4 128.6 %all-reduce.1 = (f32[128]{0:T(128)S(1)}, f32[128]{0:T(128)S(1)}, f32[128]{0:T(128)S(1)}) all-reduce(f32[128]{0:T(128)S(1)} %exponential_multiply_fusion, f32[128]{0:T(128)S(1)} %get-tuple-element.18, f32[128]{0:T(128)S(1)} %get-tuple-element.16), channel_id=1, replica_groups=mesh['vocab'=64,'tok'=8] {'vocab'}, use_global_device_ids=true, to_apply=%region_3.4 | all-reduce | flops 384 | bytes 3072 | tf_op jit(solution)/shard_map/psum | solution.py:59
  408.0 0.5 subtract_add_fusion
  408.5 0.0 copy-start.2
  408.5 0.3 fusion.10
  408.8 0.0 all-to-all-done.1
  408.8 1.9 stack.2
  410.7 0.0 copy-done.2
  410.7 4.5 all-to-all-start
  415.1 0.0 all-reduce.4.cloned.1.call-start
  415.2 8.9 %convolution_bitcast_fusion = f32[3584,128]{0,1:T(8,128)} fusion(bf16[128,1536]{1,0:T(8,128)(2,1)S(1)} %fusion.10, bf16[3584,1536]{1,0:T(8,128)(2,1)} %all-gather.2.cloned.1.call-done), kind=kOutput, calls=%fused_computation | convolution fusion | flops 1409286144 | bytes 13238272 | tf_op jit(solution)/shard_map/dot_general | solution.py:62
  424.1 0.0 all-reduce.4.cloned.1.call-update
  424.2 1.3 dynamic-slice
  426.1 192.1 %all-reduce.4.cloned.1.call-done = f32[3584,128]{0,1:T(8,128)} async-done(((f32[3584,128]{0,1:T(8,128)}), f32[3584,128]{0,1:T(8,128)}) %all-reduce.4.cloned.1.call-update) | async-done | bytes 1835024
  618.2 1.0 dynamic-slice_bitcast_fusion
  619.1 0.7 copy.14
  619.8 0.0 all-to-all-done
  619.8 4.5 fusion.1
  (3 shorter events, 0.0 us)
Async XLA Ops:
  7.2 141.3 %copy-start = (bf16[128,3584]{1,0:T(8,128)(2,1)S(1)}, bf16[128,3584]{1,0:T(8,128)(2,1)}, u32[]{:S(2)}) copy-start(bf16[128,3584]{1,0:T(8,128)(2,1)} %param.5) | copy-start | bytes 2752516
  7.2 14.5 %copy-start.3 = (s32[1,16]{1,0:T(1,128)S(1)}, s32[1,16]{1,0:T(1,128)}, u32[]{:S(2)}) copy-start(s32[1,16]{1,0:T(1,128)} %param.8) | copy-start | bytes 196
  7.2 141.2 %all-gather.2.cloned.1.call-start = ((), (), s32[]{:S(2)}) async-start(), calls=%async_computation.2 | async-start | bytes 12386304 | tf_op jit(solution)/shard_map/all_gather | solution.py:50
  10.1 398.6 %all-to-all-start.1 = ((bf16[128,8,448]{0,2,1:T(8,128)(2,1)}), bf16[128,8,448]{0,2,1:T(8,128)(2,1)S(1)}, u32[]{:S(2)}, u32[]{:S(2)}) async-start(bf16[128,8,448]{0,2,1:T(8,128)(2,1)} %bitcast.4), calls=%async_computation.1 | async-start | bytes 1835008 | tf_op jit(solution)/shard_map/all_to_all | solution.py:69
  21.8 257.1 %copy-start.1 = (bf16[128,1536]{1,0:T(8,128)(2,1)S(1)}, bf16[128,1536]{1,0:T(8,128)(2,1)}, u32[]{:S(2)}) copy-start(bf16[128,1536]{1,0:T(8,128)(2,1)} %param.7) | copy-start | bytes 1179652
  408.5 2.2 copy-start.2
  410.7 209.2 %all-to-all-start = ((bf16[8,128,1536]{2,1,0:T(8,128)(2,1)}), bf16[8,128,1536]{2,1,0:T(8,128)(2,1)}, u32[]{:S(2)}, u32[]{:S(2)}) async-start(bf16[8,128,1536]{2,1,0:T(8,128)(2,1)} %stack.2), calls=%async_computation | async-start | bytes 6291456 | tf_op jit(solution)/shard_map/all_to_all | solution.py:13
  415.1 203.0 %all-reduce.4.cloned.1.call-start = ((), (), s32[]{:S(2)}) async-start(), calls=%async_computation.3 | async-start | bytes 3670016
Sparse Core Ops, SparseCore 0:
  10.1 138.3 all-gather.1
  424.3 193.8 all-reduce.3
